TPU v7x, 32 devices: a whole 2x2x4 slice. The times are simulated.
32 devices in a mesh: groups: 2 (over y), blk: 4 (over z), uly: 2 (over x), cfg: 2 (over core).
Axes of the slice: x: 2, y: 2, z: 4, core: 2. Of those that a mesh axis runs over, the one named last changes fastest.
Arguments:
- query_rows: bfloat16 [2, 1024, 1536], P('cfg', ('groups', 'blk', 'uly')), parts along dimension 1, may hold values from -6 to 6
- key_rows: bfloat16 [2, 1024, 1536], P('cfg', ('groups', 'blk', 'uly')), parts along dimension 1, may hold values from -6 to 6
- value_rows: bfloat16 [2, 1024, 1536], P('cfg', ('groups', 'blk', 'uly')), parts along dimension 1, may hold values from -6 to 6
Outputs:
- attended: bfloat16 [2, 1024, 1536], P('cfg', ('groups', 'blk', 'uly')), parts along dimension 1
There are 2 independent parts, one for each index of `groups`. A program takes and returns all parts, laid end to end along the dimension named above; each array names one. Nothing has to cross between parts.
All inputs are finite; a program needn't handle non-finite values.
Results may differ from a plain program's by a relative error of at most 0.0045.
Values may be sent and summed in bfloat16 or wider, within the bound.
A program may use at most 128 MiB of HBM per device.

v0:
```python
import math
import jax
import jax.numpy as jnp
from jax import lax
from jax.sharding import PartitionSpec as P

HD = 128


def attend(queries, key_part, value_part):
    query_mat = queries[0, :, 0]
    row_count, head_count, head_size = query_mat.shape
    score_scale = 1.0 / math.sqrt(head_size)
    start_state = (
        jnp.full((head_count, row_count), -1e30, jnp.float32),
        jnp.zeros((head_count, row_count), jnp.float32),
        jnp.zeros((row_count, head_count, head_size), jnp.float32),
    )

    def absorb(state, pieces):
        key_piece = pieces[0][0, :, 0]
        value_piece = pieces[1][0, :, 0]
        scores = (
            jnp.einsum("qhd,khd->hqk", query_mat, key_piece, preferred_element_type=jnp.float32)
            * score_scale
        )
        running, totals, accumulated = state
        new_max = jnp.maximum(running, jnp.max(scores, axis=2))
        weights = jnp.exp(scores - new_max[:, :, None])
        factor = jnp.exp(running - new_max)
        totals = totals * factor + jnp.sum(weights, axis=2)
        probabilities = weights.astype(jnp.bfloat16)
        contrib = jnp.einsum(
            "hqk,khd->qhd", probabilities, value_piece, preferred_element_type=jnp.float32
        )
        accumulated = accumulated * factor.T[:, :, None] + contrib
        return (new_max, totals, accumulated)

    whole_keys, whole_values = (
        lax.all_gather(key_part, "blk", axis=1, tiled=True),
        lax.all_gather(value_part, "blk", axis=1, tiled=True),
    )
    key_count = whole_keys.shape[1]
    block_rows = math.gcd(key_count, 1024)

    def one_block(state, counter):
        offset = counter * block_rows
        key_block = lax.dynamic_slice_in_dim(whole_keys, offset, block_rows, 1)
        value_block = lax.dynamic_slice_in_dim(whole_values, offset, block_rows, 1)
        return (absorb(state, (key_block, value_block)), None)

    result, unused = lax.scan(
        one_block, start_state, jnp.arange(key_count // block_rows, dtype=jnp.int32)
    )
    output = (result[2] / result[1].T[:, :, None]).astype(jnp.bfloat16)
    return output.reshape(1, row_count, 1, head_count, head_size)


def regroup_back(attended_part):
    return lax.all_to_all(attended_part, "uly", split_axis=1, concat_axis=2, tiled=True)


def whole_pass(triple):
    return regroup_back(attend(triple[0], triple[1], triple[2]))


def local(query_rows, key_rows, value_rows):
    ulysses = lax.axis_size("uly")
    tokens = query_rows.shape[1]
    width = query_rows.shape[2]
    heads_local = width // HD // ulysses

    def split_heads(array):
        return array.reshape(1, tokens, ulysses, heads_local, HD)

    sectioned = (split_heads(query_rows), split_heads(key_rows), split_heads(value_rows))
    moved = (
        lax.all_to_all(sectioned[0], "uly", split_axis=2, concat_axis=1, tiled=True),
        lax.all_to_all(sectioned[1], "uly", split_axis=2, concat_axis=1, tiled=True),
        lax.all_to_all(sectioned[2], "uly", split_axis=2, concat_axis=1, tiled=True),
    )
    merged = whole_pass(moved)
    return merged.reshape(1, tokens, width)


def solution(mesh):
    in_specs = (
        P("cfg", ("groups", "blk", "uly"), None),
        P("cfg", ("groups", "blk", "uly"), None),
        P("cfg", ("groups", "blk", "uly"), None),
    )
    out_specs = P("cfg", ("groups", "blk", "uly"), None)
    return jax.shard_map(local, mesh=mesh, in_specs=in_specs, out_specs=out_specs, check_vma=False)
```

profile of v0, /device:TPU:0, one launch (start us, length us, event | category | flops | bytes accessed | tf_op | source)
XLA Modules:
  0.0 69.2 jit_solution(18183577460159070147)
XLA Ops:
  0.0 0.0 copy-start
  0.0 1.2 %reshape.23 = bf16[1,64,2,6,128]{4,3,2,1,0:T(8,128)(2,1)S(1)} reshape(bf16[1,64,1536]{2,1,0:T(8,128)(2,1)} %param.4) | data formatting | bytes 393216 | tf_op jit(solution)/shard_map/reshape | solution.py:74
  1.2 0.7 %copy.14 = bf16[1,64,2,6,128]{4,1,3,0,2:T(8,128)(2,1)} copy(bf16[1,64,2,6,128]{4,3,2,1,0:T(8,128)(2,1)S(1)} %reshape.23) | data formatting | bytes 393216 | tf_op jit(solution)/shard_map/reshape | solution.py:74
  1.9 4.2 %all-to-all-start.1 = ((bf16[1,64,2,6,128]{4,1,3,0,2:T(8,128)(2,1)}), bf16[1,64,2,6,128]{4,1,3,0,2:T(8,128)(2,1)S(1)}, u32[]{:S(2)}, u32[]{:S(2)}) async-start(bf16[1,64,2,6,128]{4,1,3,0,2:T(8,128)(2,1)} %copy.14), calls=%async_computation.1 | async-start | bytes 393216 | tf_op jit(solution)/shard_map/all_to_all | solution.py:79
  6.2 1.2 %reshape.22 = bf16[1,64,2,6,128]{4,3,2,1,0:T(8,128)(2,1)S(1)} reshape(bf16[1,64,1536]{2,1,0:T(8,128)(2,1)} %param.3) | data formatting | bytes 393216 | tf_op jit(solution)/shard_map/reshape | solution.py:74
  7.3 0.7 %copy.12 = bf16[1,64,2,6,128]{4,1,3,0,2:T(8,128)(2,1)} copy(bf16[1,64,2,6,128]{4,3,2,1,0:T(8,128)(2,1)S(1)} %reshape.22) | data formatting | bytes 393216 | tf_op jit(solution)/shard_map/reshape | solution.py:74
  8.1 0.0 copy-done
  8.1 0.2 reshape.24
  8.3 0.7 %copy.16 = bf16[1,64,2,6,128]{4,1,3,0,2:T(8,128)(2,1)} copy(bf16[1,64,2,6,128]{4,3,2,1,0:T(8,128)(2,1)S(1)} %reshape.24) | data formatting | bytes 393216 | tf_op jit(solution)/shard_map/reshape | solution.py:74
  9.0 2.3 %all-to-all-done.1 = bf16[1,64,2,6,128]{4,1,3,0,2:T(8,128)(2,1)S(1)} async-done(((bf16[1,64,2,6,128]{4,1,3,0,2:T(8,128)(2,1)}), bf16[1,64,2,6,128]{4,1,3,0,2:T(8,128)(2,1)S(1)}, u32[]{:S(2)}, u32[]{:S(2)}) %all-to-all-start.1) | async-done | bytes 196640 | tf_op jit(solution)/shard_map/all_to_all | solution.py:79
  11.3 3.4 %all-to-all-start = ((bf16[1,64,2,6,128]{4,1,3,0,2:T(8,128)(2,1)}), bf16[1,64,2,6,128]{4,1,3,0,2:T(8,128)(2,1)S(1)}, u32[]{:S(2)}, u32[]{:S(2)}) async-start(bf16[1,64,2,6,128]{4,1,3,0,2:T(8,128)(2,1)} %copy.12), calls=%async_computation | async-start | bytes 393216 | tf_op jit(solution)/shard_map/all_to_all | solution.py:78
  14.8 20.0 %all_gather.6 = bf16[1,512,1,6,128]{4,1,3,2,0:T(8,128)(2,1)S(1)} all-gather(bf16[1,128,1,6,128]{4,1,3,2,0:T(8,128)(2,1)S(1)} %bitcast.51), channel_id=1, replica_groups=mesh['groups'=2,'blk'=4,'uly'=2,'cfg'=2] {'blk'}, dimensions={1}, use_global_device_ids=true | all-gather | bytes 983040 | tf_op jit(solution)/shard_map/all_gather | solution.py:40
  34.8 0.0 all-to-all-done
  34.8 3.4 %all-to-all-start.2 = ((bf16[1,64,2,6,128]{4,1,3,0,2:T(8,128)(2,1)}), bf16[1,64,2,6,128]{4,1,3,0,2:T(8,128)(2,1)S(1)}, u32[]{:S(2)}, u32[]{:S(2)}) async-start(bf16[1,64,2,6,128]{4,1,3,0,2:T(8,128)(2,1)} %copy.16), calls=%async_computation.2 | async-start | bytes 393216 | tf_op jit(solution)/shard_map/all_to_all | solution.py:80
  38.2 0.4 fusion.10
  38.7 0.5 fusion
  39.2 3.8 %all-to-all-done.2 = bf16[1,64,2,6,128]{4,1,3,0,2:T(8,128)(2,1)S(1)} async-done(((bf16[1,64,2,6,128]{4,1,3,0,2:T(8,128)(2,1)}), bf16[1,64,2,6,128]{4,1,3,0,2:T(8,128)(2,1)S(1)}, u32[]{:S(2)}, u32[]{:S(2)}) %all-to-all-start.2) | async-done | bytes 196640 | tf_op jit(solution)/shard_map/all_to_all | solution.py:80
  43.0 17.0 %all_gather.7 = bf16[1,512,1,6,128]{4,1,3,2,0:T(8,128)(2,1)S(1)} all-gather(bf16[1,128,1,6,128]{4,1,3,2,0:T(8,128)(2,1)S(1)} %bitcast.52), channel_id=1, replica_groups=mesh['groups'=2,'blk'=4,'uly'=2,'cfg'=2] {'blk'}, dimensions={1}, use_global_device_ids=true | all-gather | bytes 983040 | tf_op jit(solution)/shard_map/all_gather | solution.py:41
  60.0 0.5 fusion.5
  60.6 0.1 copy.18
  60.7 7.6 %all_to_all.66 = bf16[1,128,1,6,128]{4,3,2,0,1:T(8,128)(2,1)S(1)} all-to-all(bf16[1,128,1,6,128]{4,3,2,0,1:T(8,128)(2,1)S(1)} %copy.18), channel_id=1, replica_groups=mesh['groups'=2,'blk'=4,'uly'=2,'cfg'=2] {'uly'}, dimensions={1} | all-to-all | bytes 393216 | tf_op jit(solution)/shard_map/all_to_all | solution.py:60
  68.3 0.9 %reshape.26 = bf16[1,64,1536]{2,1,0:T(8,128)(2,1)} reshape(bf16[1,64,2,1,6,128]{5,4,2,1,3,0:T(8,128)(2,1)S(1)} %bitcast.45) | data formatting | bytes 393216 | tf_op jit(solution)/shard_map/reshape | solution.py:83
  (6 shorter events, 0.1 us)
Async XLA Ops:
  0.0 8.1 %copy-start = (bf16[1,64,1536]{2,1,0:T(8,128)(2,1)S(1)}, bf16[1,64,1536]{2,1,0:T(8,128)(2,1)}, u32[]{:S(2)}) copy-start(bf16[1,64,1536]{2,1,0:T(8,128)(2,1)} %param.5) | copy-start | bytes 589828
  1.9 9.4 %all-to-all-start.1 = ((bf16[1,64,2,6,128]{4,1,3,0,2:T(8,128)(2,1)}), bf16[1,64,2,6,128]{4,1,3,0,2:T(8,128)(2,1)S(1)}, u32[]{:S(2)}, u32[]{:S(2)}) async-start(bf16[1,64,2,6,128]{4,1,3,0,2:T(8,128)(2,1)} %copy.14), calls=%async_computation.1 | async-start | bytes 393216 | tf_op jit(solution)/shard_map/all_to_all | solution.py:79
  11.3 23.5 %all-to-all-start = ((bf16[1,64,2,6,128]{4,1,3,0,2:T(8,128)(2,1)}), bf16[1,64,2,6,128]{4,1,3,0,2:T(8,128)(2,1)S(1)}, u32[]{:S(2)}, u32[]{:S(2)}) async-start(bf16[1,64,2,6,128]{4,1,3,0,2:T(8,128)(2,1)} %copy.12), calls=%async_computation | async-start | bytes 393216 | tf_op jit(solution)/shard_map/all_to_all | solution.py:78
  34.8 8.2 %all-to-all-start.2 = ((bf16[1,64,2,6,128]{4,1,3,0,2:T(8,128)(2,1)}), bf16[1,64,2,6,128]{4,1,3,0,2:T(8,128)(2,1)S(1)}, u32[]{:S(2)}, u32[]{:S(2)}) async-start(bf16[1,64,2,6,128]{4,1,3,0,2:T(8,128)(2,1)} %copy.16), calls=%async_computation.2 | async-start | bytes 393216 | tf_op jit(solution)/shard_map/all_to_all | solution.py:80
where the time goes:
time: 69.6 us; the launch traced here: 69.2 us
  blocking collectives  44.5 us (64%)
  starting transfers between devices  11.1 us (16%)
  waiting for transfers between devices  6.09 us (9%)
  local copies, waits for them, and re-layouts  5.94 us (9%)
  matrix products  0.98 us (1%)
    all_gather x1, blocking collectives, attend(): lax.all_gather(key_part, 'blk', axis=1, tiled=True)  20 us
    all_gather x1, blocking collectives, attend(): lax.all_gather(value_part, 'blk', axis=1, tiled=True)  17 us
    all_to_all x1, blocking collectives, regroup_back(): lax.all_to_all(attended_part, 'uly', split_axis=1, concat_axis=2, tiled=T...  7.56 us
    reshape x6, local copies, waits for them, and re-layouts, split_heads(): return array.reshape(1, tokens, ulysses, heads_local, HD)  4.8 us
    all_to_all x1, starting transfers between devices, local(): lax.all_to_all(sectioned[1], 'uly', split_axis=2, concat_axis=1, tiled=True)  4.23 us
    all_to_all x1, waiting for transfers between devices, local(): lax.all_to_all(sectioned[2], 'uly', split_axis=2, concat_axis=1, tiled=True)  3.81 us
    all_to_all x1, starting transfers between devices, local(): lax.all_to_all(sectioned[2], 'uly', split_axis=2, concat_axis=1, tiled=True)  3.43 us
    all_to_all x1, starting transfers between devices, local(): lax.all_to_all(sectioned[0], 'uly', split_axis=2, concat_axis=1, tiled=True)  3.43 us
  transfers between devices with their start and end apart: 3, of which 2 were waited for; matrix products, arithmetic and copies ran while one was open for 6% of the time, Pallas kernels for 0%

commit v1 on v0

--- a/solution.py
+++ b/solution.py
@@ -1,10 +1,38 @@
+import functools
 import math
 import jax
 import jax.numpy as jnp
 from jax import lax
 from jax.sharding import PartitionSpec as P
+from jax.lax import axis_index, axis_size, ppermute
 
 HD = 128
+
+
+def draw_the_arrays(block_here, in_dim):
+    ready = axis_size("blk")
+    y2, found_now, view_out = (ready, axis_index("blk"), block_here.shape[in_dim])
+    blocks_here = [(ii, (ii + 1) % y2) for ii in range(y2)]
+    y = jnp.zeros(
+        (*block_here.shape[:in_dim], y2 * view_out, *block_here.shape[in_dim + 1 :]),
+        block_here.dtype,
+    )
+    parts_seen = [(ii, (ii - 1) % y2) for ii in range(y2)]
+    y = lax.dynamic_update_slice_in_dim(y, block_here, found_now * view_out, axis=in_dim)
+    known = y2 // 2
+    res = spare = block_here
+    for m in [*range(1, known + 1)]:
+        res = ppermute(res, "blk", blocks_here)
+        y = lax.dynamic_update_slice_in_dim(y, res, (found_now - m) % y2 * view_out, axis=in_dim)
+        if m < y2 - known:
+            spare = ppermute(spare, "blk", parts_seen)
+            y = lax.dynamic_update_slice_in_dim(
+                y, spare, (found_now + m) % y2 * view_out, axis=in_dim
+            )
+    return y
+
+
+find_things_now = functools.partial(draw_the_arrays, in_dim=1)
 
 
 def attend(queries, key_part, value_part):
@@ -38,7 +66,7 @@
 
     whole_keys, whole_values = (
         lax.all_gather(key_part, "blk", axis=1, tiled=True),
-        lax.all_gather(value_part, "blk", axis=1, tiled=True),
+        find_things_now(value_part),
     )
     key_count = whole_keys.shape[1]
     block_rows = math.gcd(key_count, 1024)

time: 69.6 us -> 64.3 us (0.924)
  blocking collectives: 44.5 us -> 27.3 us
  waiting for transfers between devices: 6.09 us -> 10.7 us
  starting transfers between devices: 11.1 us -> 15.3 us
  local copies, waits for them, and re-layouts: 5.94 us -> 8.92 us
    all_gather x1 -> x0, blocking collectives: 17 us -> none  [attend(): lax.all_gather(value_part, 'blk', axis=1, tiled=True)]
    ppermute x0 -> x3, waiting for transfers between devices: none -> 7.44 us  [the longest x2 7.44 us: draw_the_arrays(): res = ppermute(res, 'blk', blocks_here)]
    ppermute x0 -> x3, starting transfers between devices: none -> 4.24 us  [the longest x2 2.14 us: draw_the_arrays(): res = ppermute(res, 'blk', blocks_here)]
    squeeze x0 -> x5, local copies, waits for them, and re-layouts: none -> 2.59 us  [absorb(): value_piece = pieces[1][0, :, 0]]
    all_to_all x1, waiting for transfers between devices: 2.28 us -> 0.01 us  [local(): lax.all_to_all(sectioned[1], 'uly', split_axis=2, concat_axis=1, tiled=True)]
    all_to_all x1, starting transfers between devices: 4.23 us -> 3.43 us  [local(): lax.all_to_all(sectioned[1], 'uly', split_axis=2, concat_axis=1, tiled=True)]
    all_to_all x1, starting transfers between devices: 3.43 us -> 4.23 us  [local(): lax.all_to_all(sectioned[2], 'uly', split_axis=2, concat_axis=1, tiled=True)]
  transfers between devices with their start and end apart: 3 -> 6, of which waited for: 2 -> 2; matrix products, arithmetic and copies ran while one was open for 6% -> 8% of each run, Pallas kernels for 0% -> 0%
where the time goes in v1:
time: 64.3 us; the launch traced here: 63.9 us
  blocking collectives  27.3 us (42%)
  starting transfers between devices  15.3 us (24%)
  waiting for transfers between devices  10.7 us (17%)
  local copies, waits for them, and re-layouts  8.92 us (14%)
  matrix products  0.91 us (1%)
    all_gather x1, blocking collectives, attend(): lax.all_gather(key_part, 'blk', axis=1, tiled=True)  19.3 us
    all_to_all x1, blocking collectives, regroup_back(): lax.all_to_all(attended_part, 'uly', split_axis=1, concat_axis=2, tiled=T...  7.97 us
    ppermute x2, waiting for transfers between devices, draw_the_arrays(): res = ppermute(res, 'blk', blocks_here)  7.44 us
    reshape x6, local copies, waits for them, and re-layouts, split_heads(): return array.reshape(1, tokens, ulysses, heads_local, HD)  4.81 us
    all_to_all x1, starting transfers between devices, local(): lax.all_to_all(sectioned[2], 'uly', split_axis=2, concat_axis=1, tiled=True)  4.23 us
    all_to_all x1, starting transfers between devices, local(): lax.all_to_all(sectioned[0], 'uly', split_axis=2, concat_axis=1, tiled=True)  3.43 us
    all_to_all x1, starting transfers between devices, local(): lax.all_to_all(sectioned[1], 'uly', split_axis=2, concat_axis=1, tiled=True)  3.43 us
    all_to_all x1, waiting for transfers between devices, local(): lax.all_to_all(sectioned[2], 'uly', split_axis=2, concat_axis=1, tiled=True)  3.25 us
  transfers between devices with their start and end apart: 6, of which 2 were waited for; matrix products, arithmetic and copies ran while one was open for 8% of the time, Pallas kernels for 0%

profile of v1, /device:TPU:0, one launch (start us, length us, event | category | flops | bytes accessed | tf_op | source)
XLA Modules:
  0.0 63.9 jit_solution(4928422299912232916)
XLA Ops:
  0.0 0.0 copy-start
  0.0 1.2 %reshape.33 = bf16[1,64,2,6,128]{4,3,2,1,0:T(8,128)(2,1)S(1)} reshape(bf16[1,64,1536]{2,1,0:T(8,128)(2,1)} %param.5) | data formatting | bytes 393216 | tf_op jit(solution)/shard_map/reshape | solution.py:102
  1.2 0.7 %copy.23 = bf16[1,64,2,6,128]{4,1,3,0,2:T(8,128)(2,1)} copy(bf16[1,64,2,6,128]{4,3,2,1,0:T(8,128)(2,1)S(1)} %reshape.33) | data formatting | bytes 393216 | tf_op jit(solution)/shard_map/reshape | solution.py:102
  1.9 4.2 %all-to-all-start.2 = ((bf16[1,64,2,6,128]{4,1,3,0,2:T(8,128)(2,1)}), bf16[1,64,2,6,128]{4,1,3,0,2:T(8,128)(2,1)S(1)}, u32[]{:S(2)}, u32[]{:S(2)}) async-start(bf16[1,64,2,6,128]{4,1,3,0,2:T(8,128)(2,1)} %copy.23), calls=%async_computation.2 | async-start | bytes 393216 | tf_op jit(solution)/shard_map/all_to_all | solution.py:108
  6.2 1.2 %reshape.32 = bf16[1,64,2,6,128]{4,3,2,1,0:T(8,128)(2,1)S(1)} reshape(bf16[1,64,1536]{2,1,0:T(8,128)(2,1)} %param.4) | data formatting | bytes 393216 | tf_op jit(solution)/shard_map/reshape | solution.py:102
  7.3 0.7 %copy.21 = bf16[1,64,2,6,128]{4,1,3,0,2:T(8,128)(2,1)} copy(bf16[1,64,2,6,128]{4,3,2,1,0:T(8,128)(2,1)S(1)} %reshape.32) | data formatting | bytes 393216 | tf_op jit(solution)/shard_map/reshape | solution.py:102
  8.1 3.2 %all-to-all-done.2 = bf16[1,64,2,6,128]{4,1,3,0,2:T(8,128)(2,1)S(1)} async-done(((bf16[1,64,2,6,128]{4,1,3,0,2:T(8,128)(2,1)}), bf16[1,64,2,6,128]{4,1,3,0,2:T(8,128)(2,1)S(1)}, u32[]{:S(2)}, u32[]{:S(2)}) %all-to-all-start.2) | async-done | bytes 196640 | tf_op jit(solution)/shard_map/all_to_all | solution.py:108
  11.3 3.4 %all-to-all-start.1 = ((bf16[1,64,2,6,128]{4,1,3,0,2:T(8,128)(2,1)}), bf16[1,64,2,6,128]{4,1,3,0,2:T(8,128)(2,1)S(1)}, u32[]{:S(2)}, u32[]{:S(2)}) async-start(bf16[1,64,2,6,128]{4,1,3,0,2:T(8,128)(2,1)} %copy.21), calls=%async_computation.1 | async-start | bytes 393216 | tf_op jit(solution)/shard_map/all_to_all | solution.py:107
  14.8 0.0 copy-done
  14.8 0.2 reshape.31
  15.1 0.7 %copy.19 = bf16[1,64,2,6,128]{4,1,3,0,2:T(8,128)(2,1)} copy(bf16[1,64,2,6,128]{4,3,2,1,0:T(8,128)(2,1)S(1)} %reshape.31) | data formatting | bytes 393216 | tf_op jit(solution)/shard_map/reshape | solution.py:102
  15.8 2.0 %collective-permute-start = (bf16[1,128,1,6,128]{4,1,3,2,0:T(8,128)(2,1)S(1)}, bf16[1,128,1,6,128]{4,1,3,2,0:T(8,128)(2,1)}, u32[]{:S(2)}, u32[]{:S(2)}) collective-permute-start(bf16[1,128,1,6,128]{4,1,3,2,0:T(8,128)(2,1)S(1)} %bitcast.51), channel_id=1, source_target_pairs={{0,4},{4,8},{8,12},{12,0},{1,5},{5,9},{9,13},{13,1},{2,6},{6,10},{... | collective-permute-start | bytes 589832 | tf_op jit(solution)/shard_map/ppermute | solution.py:25
  17.8 2.1 %collective-permute-start.1 = (bf16[1,128,1,6,128]{4,1,3,2,0:T(8,128)(2,1)S(1)}, bf16[1,128,1,6,128]{4,1,3,2,0:T(8,128)(2,1)}, u32[]{:S(2)}, u32[]{:S(2)}) collective-permute-start(bf16[1,128,1,6,128]{4,1,3,2,0:T(8,128)(2,1)S(1)} %bitcast.52), channel_id=1, source_target_pairs={{0,12},{4,0},{8,4},{12,8},{1,13},{5,1},{9,5},{13,9},{2,14},{6,2},{... | collective-permute-start | bytes 589832 | tf_op jit(solution)/shard_map/ppermute | solution.py:28
  19.9 0.0 all-to-all-done.1
  19.9 3.4 %all-to-all-start = ((bf16[1,64,2,6,128]{4,1,3,0,2:T(8,128)(2,1)}), bf16[1,64,2,6,128]{4,1,3,0,2:T(8,128)(2,1)S(1)}, u32[]{:S(2)}, u32[]{:S(2)}) async-start(bf16[1,64,2,6,128]{4,1,3,0,2:T(8,128)(2,1)} %copy.19), calls=%async_computation | async-start | bytes 393216 | tf_op jit(solution)/shard_map/all_to_all | solution.py:106
  23.4 19.3 %all_gather.3 = bf16[1,512,1,6,128]{4,1,3,2,0:T(8,128)(2,1)S(1)} all-gather(bf16[1,128,1,6,128]{4,1,3,2,0:T(8,128)(2,1)S(1)} %bitcast.55), channel_id=1, replica_groups=mesh['groups'=2,'blk'=4,'uly'=2,'cfg'=2] {'blk'}, dimensions={1}, use_global_device_ids=true | all-gather | bytes 983040 | tf_op jit(solution)/shard_map/all_gather | solution.py:68
  42.7 0.2 copy.25
  42.9 0.0 all-to-all-done
  42.9 0.4 fusion.9
  43.4 0.5 fusion
  43.9 0.1 squeeze.24
  43.9 0.1 constant_dynamic-update-slice_fusion.3
  44.0 0.0 collective-permute-done
  44.0 1.1 %copy.26 = bf16[128,6,128]{0,2,1:T(8,128)(2,1)S(1)} copy(bf16[128,6,128]{2,0,1:T(8,128)(2,1)} %bitcast.13) | data formatting | bytes 393216 | tf_op jit(solution)/shard_map/while/body/eval_jaxpr/squeeze | solution.py:50
  45.1 0.0 collective-permute-done.1
  45.1 1.1 %copy.27 = bf16[128,6,128]{0,2,1:T(8,128)(2,1)S(1)} copy(bf16[128,6,128]{2,0,1:T(8,128)(2,1)} %bitcast.15) | data formatting | bytes 393216 | tf_op jit(solution)/shard_map/while/body/eval_jaxpr/squeeze | solution.py:50
  46.2 0.2 collective-permute-start.2
  46.5 0.1 constant_dynamic-update-slice_fusion.1
  46.5 7.4 %collective-permute-done.2 = bf16[1,128,1,6,128]{4,1,3,2,0:T(8,128)(2,1)S(1)} collective-permute-done((bf16[1,128,1,6,128]{4,1,3,2,0:T(8,128)(2,1)}, bf16[1,128,1,6,128]{4,1,3,2,0:T(8,128)(2,1)S(1)}, u32[]{:S(2)}, u32[]{:S(2)}) %collective-permute-start.2) | collective-permute-done | bytes 196640 | tf_op jit(solution)/shard_map/ppermute | solution.py:25
  53.9 0.2 copy.28
  54.1 0.1 constant_dynamic-update-slice_fusion
  54.2 0.5 fusion.5
  54.6 0.2 copy.29
  54.8 8.0 %all_to_all.66 = bf16[1,128,1,6,128]{4,3,2,0,1:T(8,128)(2,1)S(1)} all-to-all(bf16[1,128,1,6,128]{4,3,2,0,1:T(8,128)(2,1)S(1)} %copy.29), channel_id=1, replica_groups=mesh['groups'=2,'blk'=4,'uly'=2,'cfg'=2] {'uly'}, dimensions={1} | all-to-all | bytes 393216 | tf_op jit(solution)/shard_map/all_to_all | solution.py:88
  62.8 0.1 copy.31
  63.0 0.9 %reshape.35 = bf16[1,64,1536]{2,1,0:T(8,128)(2,1)} reshape(bf16[1,64,2,1,6,128]{5,4,2,1,3,0:T(8,128)(2,1)S(1)} %copy.31) | data formatting | bytes 393216 | tf_op jit(solution)/shard_map/reshape | solution.py:111
  (7 shorter events, 0.1 us)
Async XLA Ops:
  0.0 14.8 %copy-start = (bf16[1,64,1536]{2,1,0:T(8,128)(2,1)S(1)}, bf16[1,64,1536]{2,1,0:T(8,128)(2,1)}, u32[]{:S(2)}) copy-start(bf16[1,64,1536]{2,1,0:T(8,128)(2,1)} %param.3) | copy-start | bytes 589828
  1.9 9.4 %all-to-all-start.2 = ((bf16[1,64,2,6,128]{4,1,3,0,2:T(8,128)(2,1)}), bf16[1,64,2,6,128]{4,1,3,0,2:T(8,128)(2,1)S(1)}, u32[]{:S(2)}, u32[]{:S(2)}) async-start(bf16[1,64,2,6,128]{4,1,3,0,2:T(8,128)(2,1)} %copy.23), calls=%async_computation.2 | async-start | bytes 393216 | tf_op jit(solution)/shard_map/all_to_all | solution.py:108
  11.3 8.6 %all-to-all-start.1 = ((bf16[1,64,2,6,128]{4,1,3,0,2:T(8,128)(2,1)}), bf16[1,64,2,6,128]{4,1,3,0,2:T(8,128)(2,1)S(1)}, u32[]{:S(2)}, u32[]{:S(2)}) async-start(bf16[1,64,2,6,128]{4,1,3,0,2:T(8,128)(2,1)} %copy.21), calls=%async_computation.1 | async-start | bytes 393216 | tf_op jit(solution)/shard_map/all_to_all | solution.py:107
  15.8 28.2 %collective-permute-start = (bf16[1,128,1,6,128]{4,1,3,2,0:T(8,128)(2,1)S(1)}, bf16[1,128,1,6,128]{4,1,3,2,0:T(8,128)(2,1)}, u32[]{:S(2)}, u32[]{:S(2)}) collective-permute-start(bf16[1,128,1,6,128]{4,1,3,2,0:T(8,128)(2,1)S(1)} %bitcast.51), channel_id=1, source_target_pairs={{0,4},{4,8},{8,12},{12,0},{1,5},{5,9},{9,13},{13,1},{2,6},{6,10},{... | collective-permute-start | bytes 589832 | tf_op jit(solution)/shard_map/ppermute | solution.py:25
  17.8 27.3 %collective-permute-start.1 = (bf16[1,128,1,6,128]{4,1,3,2,0:T(8,128)(2,1)S(1)}, bf16[1,128,1,6,128]{4,1,3,2,0:T(8,128)(2,1)}, u32[]{:S(2)}, u32[]{:S(2)}) collective-permute-start(bf16[1,128,1,6,128]{4,1,3,2,0:T(8,128)(2,1)S(1)} %bitcast.52), channel_id=1, source_target_pairs={{0,12},{4,0},{8,4},{12,8},{1,13},{5,1},{9,5},{13,9},{2,14},{6,2},{... | collective-permute-start | bytes 589832 | tf_op jit(solution)/shard_map/ppermute | solution.py:28
  19.9 23.0 %all-to-all-start = ((bf16[1,64,2,6,128]{4,1,3,0,2:T(8,128)(2,1)}), bf16[1,64,2,6,128]{4,1,3,0,2:T(8,128)(2,1)S(1)}, u32[]{:S(2)}, u32[]{:S(2)}) async-start(bf16[1,64,2,6,128]{4,1,3,0,2:T(8,128)(2,1)} %copy.19), calls=%async_computation | async-start | bytes 393216 | tf_op jit(solution)/shard_map/all_to_all | solution.py:106
  46.2 7.7 %collective-permute-start.2 = (bf16[1,128,1,6,128]{4,1,3,2,0:T(8,128)(2,1)}, bf16[1,128,1,6,128]{4,1,3,2,0:T(8,128)(2,1)S(1)}, u32[]{:S(2)}, u32[]{:S(2)}) collective-permute-start(bf16[1,128,1,6,128]{4,1,3,2,0:T(8,128)(2,1)} %collective-permute-done), channel_id=1, source_target_pairs={{0,4},{4,8},{8,12},{12,0},{1,5},{5,9},{9,13},{13,1},{2,6},{6,10},{... | collective-permute-start | bytes 589832 | tf_op jit(solution)/shard_map/ppermute | solution.py:25
